TPU v7x, 32 devices: a whole 2x2x4 slice. The times are simulated.
32 devices in a mesh: seq: 2 (over x), batch: 4 (over y, core), head: 4 (over z).
Axes of the slice: x: 2, y: 2, z: 4, core: 2. Of those that a mesh axis runs over, the one named last changes fastest.
Arguments:
- hidden: bfloat16 [4, 256, 16384], P('batch', None, 'seq'), may hold values from -760 to 760
- gain: float32 [16384], P('seq'), may hold values from 0.5 to 1.5
- key_weight: bfloat16 [16384, 1024], P('seq', 'head'), may hold values from -0.046875 to 0.046875
- value_weight: bfloat16 [16384, 1024], P('seq', 'head'), may hold values from -0.046875 to 0.046875
- positions: int32 [4, 256], P('batch', 'seq'), may hold values from 0 to 32767
- initial_basis: float32 [2048, 256], P('head'), may hold values from -6 to 6
Outputs:
- basis: float32 [2048, 256], P('head')
All inputs are finite; a program needn't handle non-finite values.
Results may differ from a plain program's by a relative error of at most 0.0063.
Values may be sent and summed in bfloat16 or wider, within the bound.
A program may use at most 64 MiB of HBM per device.

v0:
```python
import math

import jax
import jax.numpy as jnp
from jax import lax
from jax.sharding import PartitionSpec as P

D = 16384
HEAD_DIM = 128
ITERS = 4


EPSILON = 1e-05
ROTARY_BASE = 500000.0


def rotary(head_rows, position_row):
    half_width = head_rows.shape[-1] // 2
    index_row = jnp.arange(half_width, dtype=jnp.float32)
    frequency = jnp.exp(index_row * (-math.log(ROTARY_BASE) / half_width))
    angles = position_row.astype(jnp.float32)[:, None] * frequency[None, :]
    cosine = jnp.cos(angles)[:, None, :]
    sine_part = jnp.sin(angles)[:, None, :]
    first_half = head_rows[..., :half_width]
    second_half = head_rows[..., half_width:]
    return jnp.concatenate(
        [
            first_half * cosine - second_half * sine_part,
            second_half * cosine + first_half * sine_part,
        ],
        axis=-1,
    )


def whole_of(basis_block):
    return lax.all_gather(basis_block, "head", axis=0, tiled=True)


def total_squares(local_squares, local_tokens):
    all_squares = lax.psum(local_squares, "seq")
    return lax.dynamic_slice_in_dim(all_squares, lax.axis_index("seq") * local_tokens, local_tokens)


def gram_of(images):
    return lax.dot_general(
        images,
        images,
        (((0,), (0,)), ((), ())),
        precision=lax.Precision.HIGHEST,
        preferred_element_type=jnp.float32,
    )


def orthonormal(images, gram_matrix):
    factor = jnp.linalg.cholesky(gram_matrix)
    return lax.linalg.triangular_solve(
        factor, images, left_side=False, lower=True, transpose_a=True
    )


def body(hidden, gain, key_weight, value_weight, positions, initial_basis):
    hidden_rows = hidden[0]
    local_tokens = positions.shape[1]
    widened = hidden_rows.astype(jnp.float32)
    scaled = (widened * gain).astype(jnp.bfloat16)
    local_squares = jnp.sum(widened * widened, axis=1)
    key_columns = key_weight.shape[1]
    weights = jnp.concatenate([key_weight, value_weight], axis=1)
    own_squares = total_squares(local_squares, local_tokens)
    projected = lax.psum_scatter(
        jnp.dot(scaled, weights, preferred_element_type=jnp.float32),
        "seq",
        scatter_dimension=0,
        tiled=True,
    )
    inverse_scale = lax.rsqrt(own_squares / D + EPSILON)
    projected = projected * inverse_scale[:, None]
    key_rows = rotary(projected[:, :key_columns].reshape(local_tokens, -1, HEAD_DIM), positions[0])
    value_rows = projected[:, key_columns:].reshape(local_tokens, -1, HEAD_DIM)
    joint_rows = (
        jnp.stack([key_rows, value_rows], axis=2).reshape(local_tokens, -1).astype(jnp.bfloat16)
    )
    partial_value = lax.dot_general(
        joint_rows,
        lax.all_gather(joint_rows, "head", axis=1, tiled=True),
        (((0,), (0,)), ((), ())),
        preferred_element_type=jnp.float32,
    )
    token_total = local_tokens * lax.axis_size("seq") * lax.axis_size("batch")
    basis_block = initial_basis
    covariance = lax.psum(partial_value, ("seq", "batch")) / token_total
    for iteration in range(ITERS):
        whole_basis = whole_of(basis_block)
        images = jnp.dot(
            covariance,
            whole_basis,
            precision=lax.Precision.HIGHEST,
            preferred_element_type=jnp.float32,
        )
        gram_matrix = lax.psum(gram_of(images), "head") / whole_basis.shape[0]
        basis_block = orthonormal(images, gram_matrix)
    return basis_block


def solution(mesh):
    return jax.shard_map(
        body,
        mesh=mesh,
        in_specs=(
            P("batch", None, "seq"),
            P("seq"),
            P("seq", "head"),
            P("seq", "head"),
            P("batch", "seq"),
            P("head", None),
        ),
        out_specs=P("head", None),
        check_vma=False,
    )
```

profile of v0, /device:TPU:0, one launch (start us, length us, event | category | flops | bytes accessed | tf_op | source)
XLA Modules:
  0.0 706.8 jit_solution(16877559719014018275)
XLA Ops:
  7.4 7.8 %fusion.2 = f32[256,512]{1,0:T(8,128)} fusion(bf16[8192,256]{1,0:T(8,128)(2,1)} %param.12, bf16[8192,256]{1,0:T(8,128)(2,1)} %param.11, bf16[1,256,8192]{2,1,0:T(8,128)(2,1)} %param.9, f32[8192]{0:T(1024)} %param.10), kind=kOutput, calls=%fused_computation.12 | convolution fusion | flops 2170552320 | bytes 13139968 | tf_op jit(solution)/shard_map/dot_general | solution.py:71
  18.4 5.9 psum.42
  24.5 8.2 %reduce-scatter.2.cloned.1.call-done = f32[128,512]{1,0:T(8,128)} async-done(((f32[256,512]{1,0:T(8,128)}), f32[128,512]{1,0:T(8,128)}) %reduce-scatter.2.cloned.1.call-update) | async-done | bytes 262160 | tf_op jit(solution)/shard_map/reduce_scatter | solution.py:70
  34.1 15.5 %all_gather.15 = bf16[128,2048]{0,1:T(8,128)(2,1)S(1)} all-gather(bf16[128,512]{0,1:T(8,128)(2,1)S(1)} %bitcast.160), channel_id=1, replica_groups=mesh['seq'=2,'batch'=4,'head'=4] {'head'}, dimensions={1}, use_global_device_ids=true | all-gather | bytes 655360 | tf_op jit(solution)/shard_map/all_gather | solution.py:85
  52.9 81.2 %all-reduce.7.cloned.1.call-done = f32[512,2048]{1,0:T(8,128)} async-done(((f32[512,2048]{1,0:T(8,128)}), f32[512,2048]{1,0:T(8,128)}) %all-reduce.7.cloned.1.call-update) | async-done | bytes 4194320 | tf_op jit(solution)/shard_map/psum | solution.py:91
  134.1 6.1 fusion.15
  142.2 35.5 %all-reduce.9.cloned.1.call-done = f32[256,256]{0,1:T(8,128)} async-done(((f32[256,256]{0,1:T(8,128)}), f32[256,256]{0,1:T(8,128)}) %all-reduce.9.cloned.1.call-update) | async-done | bytes 262160 | tf_op jit(solution)/shard_map/psum | solution.py:100
  179.8 11.7 %cholesky.214 = f32[128,128]{1,0:T(8,128)S(1)} custom-call(f32[128,128]{1,0:T(8,128)S(1)} %cholesky.346), custom_call_target="Cholesky" | custom-call | tf_op jit(solution)/shard_map/jit(cholesky)/cholesky | solution.py:55
  191.5 9.8 %custom-call.17 = f32[1,128,128]{1,2,0:T(8,128)S(1)} custom-call(f32[1,128,128]{2,1,0:T(8,128)S(1)} %get-tuple-element.94), custom_call_target="InvertDiagBlocksLowerTriangular" | custom-call | tf_op jit(solution)/shard_map/jit(cholesky)/cholesky | solution.py:55
  201.9 11.7 %cholesky.231 = f32[128,128]{1,0:T(8,128)S(1)} custom-call(f32[128,128]{1,0:T(8,128)S(1)} %convolution_subtract_fusion.7), custom_call_target="Cholesky" | custom-call | tf_op jit(solution)/shard_map/jit(cholesky)/cholesky | solution.py:55
  219.8 19.7 %custom-call.18 = f32[2,128,128]{1,2,0:T(8,128)S(1)} custom-call(f32[2,128,128]{2,1,0:T(8,128)S(1)} %get-tuple-element.33), custom_call_target="InvertDiagBlocksLowerTriangular" | custom-call | tf_op jit(solution)/shard_map/triangular_solve/custom-call.0 | solution.py:56
  241.8 45.1 %all-gather.7.cloned.1.call-done = f32[2048,256]{0,1:T(8,128)} async-done(((f32[512,256]{0,1:T(8,128)}), f32[2048,256]{0,1:T(8,128)}) %all-gather.7.cloned.1.call-update) | async-done | bytes 2097168 | tf_op jit(solution)/shard_map/all_gather | solution.py:36
  287.0 6.1 fusion.13
  295.1 34.2 %all-reduce.11.cloned.1.call-done = f32[256,256]{0,1:T(8,128)} async-done(((f32[256,256]{0,1:T(8,128)}), f32[256,256]{0,1:T(8,128)}) %all-reduce.11.cloned.1.call-update) | async-done | bytes 262160 | tf_op jit(solution)/shard_map/psum | solution.py:100
  331.3 11.7 %cholesky.248 = f32[128,128]{1,0:T(8,128)S(1)} custom-call(f32[128,128]{1,0:T(8,128)S(1)} %cholesky.349), custom_call_target="Cholesky" | custom-call | tf_op jit(solution)/shard_map/jit(cholesky)/cholesky | solution.py:55
  343.1 9.8 %custom-call.19 = f32[1,128,128]{1,2,0:T(8,128)S(1)} custom-call(f32[1,128,128]{2,1,0:T(8,128)S(1)} %get-tuple-element.90), custom_call_target="InvertDiagBlocksLowerTriangular" | custom-call | tf_op jit(solution)/shard_map/jit(cholesky)/cholesky | solution.py:55
  353.4 11.7 %cholesky.265 = f32[128,128]{1,0:T(8,128)S(1)} custom-call(f32[128,128]{1,0:T(8,128)S(1)} %convolution_subtract_fusion.6), custom_call_target="Cholesky" | custom-call | tf_op jit(solution)/shard_map/jit(cholesky)/cholesky | solution.py:55
  372.2 19.7 %custom-call.20 = f32[2,128,128]{1,2,0:T(8,128)S(1)} custom-call(f32[2,128,128]{2,1,0:T(8,128)S(1)} %get-tuple-element.34), custom_call_target="InvertDiagBlocksLowerTriangular" | custom-call | tf_op jit(solution)/shard_map/triangular_solve/custom-call.0 | solution.py:56
  394.2 45.1 %all-gather.9.cloned.1.call-done = f32[2048,256]{0,1:T(8,128)} async-done(((f32[512,256]{0,1:T(8,128)}), f32[2048,256]{0,1:T(8,128)}) %all-gather.9.cloned.1.call-update) | async-done | bytes 2097168 | tf_op jit(solution)/shard_map/all_gather | solution.py:36
  439.3 6.1 fusion.11
  447.3 34.3 %all-reduce.13.cloned.1.call-done = f32[256,256]{0,1:T(8,128)} async-done(((f32[256,256]{0,1:T(8,128)}), f32[256,256]{0,1:T(8,128)}) %all-reduce.13.cloned.1.call-update) | async-done | bytes 262160 | tf_op jit(solution)/shard_map/psum | solution.py:100
  483.7 11.7 %cholesky.282 = f32[128,128]{1,0:T(8,128)S(1)} custom-call(f32[128,128]{1,0:T(8,128)S(1)} %cholesky.352), custom_call_target="Cholesky" | custom-call | tf_op jit(solution)/shard_map/jit(cholesky)/cholesky | solution.py:55
  495.5 9.8 %custom-call.21 = f32[1,128,128]{1,2,0:T(8,128)S(1)} custom-call(f32[1,128,128]{2,1,0:T(8,128)S(1)} %get-tuple-element.86), custom_call_target="InvertDiagBlocksLowerTriangular" | custom-call | tf_op jit(solution)/shard_map/jit(cholesky)/cholesky | solution.py:55
  505.8 11.7 %cholesky.299 = f32[128,128]{1,0:T(8,128)S(1)} custom-call(f32[128,128]{1,0:T(8,128)S(1)} %convolution_subtract_fusion.5), custom_call_target="Cholesky" | custom-call | tf_op jit(solution)/shard_map/jit(cholesky)/cholesky | solution.py:55
  524.3 19.7 %custom-call.22 = f32[2,128,128]{1,2,0:T(8,128)S(1)} custom-call(f32[2,128,128]{2,1,0:T(8,128)S(1)} %get-tuple-element.35), custom_call_target="InvertDiagBlocksLowerTriangular" | custom-call | tf_op jit(solution)/shard_map/triangular_solve/custom-call.0 | solution.py:56
  546.3 45.1 %all-gather.11.cloned.1.call-done = f32[2048,256]{0,1:T(8,128)} async-done(((f32[512,256]{0,1:T(8,128)}), f32[2048,256]{0,1:T(8,128)}) %all-gather.11.cloned.1.call-update) | async-done | bytes 2097168 | tf_op jit(solution)/shard_map/all_gather | solution.py:36
  591.4 6.1 fusion.9
  599.2 34.5 %all-reduce.15.cloned.1.call-done = f32[256,256]{0,1:T(8,128)} async-done(((f32[256,256]{0,1:T(8,128)}), f32[256,256]{0,1:T(8,128)}) %all-reduce.15.cloned.1.call-update) | async-done | bytes 262160 | tf_op jit(solution)/shard_map/psum | solution.py:100
  635.8 11.7 %cholesky.316 = f32[128,128]{1,0:T(8,128)S(1)} custom-call(f32[128,128]{1,0:T(8,128)S(1)} %cholesky.355), custom_call_target="Cholesky" | custom-call | tf_op jit(solution)/shard_map/jit(cholesky)/cholesky | solution.py:55
  647.6 9.8 %custom-call.23 = f32[1,128,128]{1,2,0:T(8,128)S(1)} custom-call(f32[1,128,128]{2,1,0:T(8,128)S(1)} %get-tuple-element.82), custom_call_target="InvertDiagBlocksLowerTriangular" | custom-call | tf_op jit(solution)/shard_map/jit(cholesky)/cholesky | solution.py:55
  657.9 11.7 %cholesky.333 = f32[128,128]{1,0:T(8,128)S(1)} custom-call(f32[128,128]{1,0:T(8,128)S(1)} %convolution_subtract_fusion.4), custom_call_target="Cholesky" | custom-call | tf_op jit(solution)/shard_map/jit(cholesky)/cholesky | solution.py:55
  676.5 19.9 %custom-call.24 = f32[2,128,128]{1,2,0:T(8,128)S(1)} custom-call(f32[2,128,128]{2,1,0:T(8,128)S(1)} %get-tuple-element.36), custom_call_target="InvertDiagBlocksLowerTriangular" | custom-call | tf_op jit(solution)/shard_map/triangular_solve/custom-call.0 | solution.py:56
  (139 shorter events, 73.0 us)
Async XLA Ops:
  7.4 25.3 %reduce-scatter.2.cloned.1.call-start = ((), (), s32[]{:S(2)}) async-start(), calls=%async_computation.1 | async-start | bytes 786432 | tf_op jit(solution)/shard_map/reduce_scatter | solution.py:70
  15.2 9.1 %copy-start = (s32[1,128]{1,0:T(1,128)S(1)}, s32[1,128]{1,0:T(1,128)}, u32[]{:S(2)}) copy-start(s32[1,128]{1,0:T(1,128)} %param.13) | copy-start | bytes 1540
  15.2 118.9 %all-reduce.7.cloned.1.call-start = ((), (), s32[]{:S(2)}) async-start(), calls=%async_computation.2 | async-start | bytes 8388608 | tf_op jit(solution)/shard_map/psum | solution.py:91
  52.3 81.8 %all-gather.5.cloned.1.call-start = ((), (), s32[]{:S(2)}) async-start(), calls=%async_computation.3 | async-start | bytes 2621440 | tf_op jit(solution)/shard_map/all_gather | solution.py:36
  52.9 124.8 %all-reduce.9.cloned.1.call-start = ((), (), s32[]{:S(2)}) async-start(), calls=%async_computation.4 | async-start | bytes 524288 | tf_op jit(solution)/shard_map/psum | solution.py:100
  141.9 145.0 %all-gather.7.cloned.1.call-start = ((), (), s32[]{:S(2)}) async-start(), calls=%async_computation.5 | async-start | bytes 2621440 | tf_op jit(solution)/shard_map/all_gather | solution.py:36
  241.8 87.4 %all-reduce.11.cloned.1.call-start = ((), (), s32[]{:S(2)}) async-start(), calls=%async_computation.6 | async-start | bytes 524288 | tf_op jit(solution)/shard_map/psum | solution.py:100
  294.7 144.6 %all-gather.9.cloned.1.call-start = ((), (), s32[]{:S(2)}) async-start(), calls=%async_computation.7 | async-start | bytes 2621440 | tf_op jit(solution)/shard_map/all_gather | solution.py:36
  394.2 87.4 %all-reduce.13.cloned.1.call-start = ((), (), s32[]{:S(2)}) async-start(), calls=%async_computation.8 | async-start | bytes 524288 | tf_op jit(solution)/shard_map/psum | solution.py:100
  447.1 144.3 %all-gather.11.cloned.1.call-start = ((), (), s32[]{:S(2)}) async-start(), calls=%async_computation.9 | async-start | bytes 2621440 | tf_op jit(solution)/shard_map/all_gather | solution.py:36
  546.3 87.4 %all-reduce.15.cloned.1.call-start = ((), (), s32[]{:S(2)}) async-start(), calls=%async_computation.10 | async-start | bytes 524288 | tf_op jit(solution)/shard_map/psum | solution.py:100
Sparse Core Ops, SparseCore 0:
  15.3 17.3 reduce-scatter.1
  52.4 81.6 all-reduce.6
Sparse Core Ops, SparseCore 1:
  54.3 46.3 all-gather.4
  142.0 35.6 all-reduce.8
  241.9 45.0 all-gather.6
  294.8 34.3 all-reduce.10
  394.3 45.0 all-gather.8
  447.2 34.3 all-reduce.12
  546.4 45.0 all-gather.10
  599.3 34.3 all-reduce.14
where the time goes:
time: 719 us; the launch traced here: 707 us
  waiting for transfers between devices  364 us (51%)
  other arithmetic  232 us (32%)
  matrix products  49.2 us (7%)
  blocking collectives  21.4 us (3%)
  between operations  21.1 us (3%)
  local copies, waits for them, and re-layouts  17.7 us (2%)
    psum x4, waiting for transfers between devices, body(): gram_matrix = lax.psum(gram_of(images), 'head') / whole_basis.shape[0]  138 us
    another operation x27, other arithmetic, orthonormal(): factor = jnp.linalg.cholesky(gram_matrix)  138 us
    all_gather x4, waiting for transfers between devices, whole_of(): return lax.all_gather(basis_block, 'head', axis=0, tiled=True)  135 us
    another operation x13, other arithmetic, orthonormal(): lax.linalg.triangular_solve(factor, images, left_side=False, lower=True,...  81.6 us
    psum x1, waiting for transfers between devices, body(): covariance = lax.psum(partial_value, ('seq', 'batch')) / token_total  81.2 us
    dot_general x4, matrix products, body(): jnp.dot(covariance, whole_basis, precision=lax.Precision.HIGHEST, preferr...  24.3 us
    another operation x30, local copies, waits for them, and re-layouts, orthonormal(): lax.linalg.triangular_solve(factor, images, left_side=False, lower=True,...  16.8 us
    all_gather x1, blocking collectives, body(): lax.all_gather(joint_rows, 'head', axis=1, tiled=True)  15.5 us
  transfers between devices with their start and end apart: 10, of which 9 were waited for; matrix products, arithmetic and copies ran while one was open for 0% of the time, Pallas kernels for 0%

commit v1 on v0

--- a/solution.py
+++ b/solution.py
@@ -3,6 +3,8 @@
 import jax
 import jax.numpy as jnp
 from jax import lax
+from jax.experimental import pallas as pl
+from jax.experimental.pallas import tpu as pltpu
 from jax.sharding import PartitionSpec as P
 
 D = 16384
@@ -58,6 +60,151 @@
     )
 
 
+LANES = 128
+SUBLANES = 8
+
+
+def dot_of(left, right, left_axis, right_axis, precision=None):
+    return lax.dot_general(
+        left,
+        right,
+        (((left_axis,), (right_axis,)), ((), ())),
+        precision=precision,
+        preferred_element_type=jnp.float32,
+    )
+
+
+def exact(left, right, left_axis, right_axis):
+    return dot_of(left, right, left_axis, right_axis, lax.Precision.HIGHEST)
+
+
+def halves_of(value):
+    high = value.astype(jnp.bfloat16)
+    return high, (value - high.astype(jnp.float32)).astype(jnp.bfloat16)
+
+
+def inverse_factor(matrix):
+    size = matrix.shape[0]
+    rows = lax.broadcasted_iota(jnp.int32, (SUBLANES, size), 0)
+    lanes = lax.broadcasted_iota(jnp.int32, (SUBLANES, size), 1)
+    groups = size // SUBLANES
+    left = [matrix[SUBLANES * g : SUBLANES * (g + 1)] for g in range(groups)]
+    right = [jnp.where(lanes == rows + SUBLANES * g, 1.0, 0.0) for g in range(groups)]
+    done = []
+
+    def spread_row(value, at):
+        return jnp.broadcast_to(value[at : at + 1, :], (SUBLANES, size))
+
+    def spread_lane(value, at):
+        return jnp.broadcast_to(value[:, at : at + 1], (SUBLANES, size))
+
+    for pivot in range(0, size, 2):
+        own, at = pivot // SUBLANES, pivot % SUBLANES
+        top, low = spread_row(left[own], at), spread_row(left[own], at + 1)
+        top_right, low_right = spread_row(right[own], at), spread_row(right[own], at + 1)
+        first, cross, last = (
+            spread_lane(top, pivot),
+            spread_lane(top, pivot + 1),
+            spread_lane(low, pivot + 1),
+        )
+        scale = 1.0 / (first * last - cross * cross)
+        mix_top = (top * last - low * cross) * scale
+        mix_low = (low * first - top * cross) * scale
+        mix_top_right = (top_right * last - low_right * cross) * scale
+        mix_low_right = (low_right * first - top_right * cross) * scale
+        ratio = cross / first
+        done.append(
+            (
+                top_right * lax.rsqrt(first),
+                (low_right - ratio * top_right) * lax.rsqrt(last - ratio * cross),
+            )
+        )
+        for g in range(own, groups):
+            if g == own and at + 2 >= SUBLANES:
+                continue
+            one, two = spread_lane(left[g], pivot), spread_lane(left[g], pivot + 1)
+            if g == own:
+                one = jnp.where(rows > at + 1, one, 0.0)
+                two = jnp.where(rows > at + 1, two, 0.0)
+            left[g] = left[g] - one * mix_top - two * mix_low
+            right[g] = right[g] - one * mix_top_right - two * mix_low_right
+    blocks = []
+    for g in range(groups):
+        block = jnp.zeros((SUBLANES, size), jnp.float32)
+        for pair in range(SUBLANES // 2):
+            upper, lower = done[g * SUBLANES // 2 + pair]
+            block = jnp.where(rows == 2 * pair, upper, block)
+            block = jnp.where(rows == 2 * pair + 1, lower, block)
+        blocks.append(block)
+    return jnp.concatenate(blocks, axis=0)
+
+
+def iterate_kernel(joint_ref, basis_ref, own_ref, out_ref, high_ref, low_ref, rows_ref, images_ref, gram_ref, inverse_ref):
+    tokens, joint = joint_ref.shape
+    rank = basis_ref.shape[1]
+    panels = rank // LANES
+    strip = 256
+    for start in range(0, tokens, strip):
+        kernel_rows = dot_of(joint_ref[start : start + strip, :], joint_ref[...], 1, 1) * (1.0 / tokens)
+        high, low = halves_of(kernel_rows)
+        high_ref[start : start + strip, :] = high
+        low_ref[start : start + strip, :] = low
+    basis_high, basis_low = halves_of(basis_ref[...])
+    rows_ref[...] = dot_of(joint_ref[...], basis_high, 1, 0) + dot_of(joint_ref[...], basis_low, 1, 0)
+
+    def step(iteration, carry):
+        rows_high, rows_low = halves_of(rows_ref[...])
+        images_ref[...] = (
+            dot_of(high_ref[...], rows_high, 1, 0)
+            + dot_of(high_ref[...], rows_low, 1, 0)
+            + dot_of(low_ref[...], rows_high, 1, 0)
+        )
+        gram_ref[...] = exact(rows_ref[...], images_ref[...], 0, 0) * (1.0 / (tokens * joint))
+
+        @pl.when(iteration < ITERS - 1)
+        def _():
+            rows_ref[...] = images_ref[...]
+
+        def panel_step(panel, inner):
+            at = pl.ds(pl.multiple_of(panel * LANES, LANES), LANES)
+            inverse = inverse_factor(gram_ref[at, at])
+            scaled = exact(inverse, gram_ref[at, :], 1, 0)
+            lane = lax.broadcasted_iota(jnp.int32, scaled.shape, 1)
+            scaled = jnp.where(lane >= (panel + 1) * LANES, scaled, 0.0)
+            gram_ref[...] -= exact(scaled, scaled, 0, 0)
+            columns = exact(rows_ref[:, at], inverse, 1, 1)
+            rows_ref[...] -= exact(columns, scaled, 1, 0)
+            rows_ref[:, at] = columns
+            return inner
+
+        lax.fori_loop(0, panels, panel_step, 0)
+        return carry
+
+    lax.fori_loop(0, ITERS, step, 0)
+    rows_high, rows_low = halves_of(rows_ref[...])
+    out_ref[...] = (dot_of(own_ref[...], rows_high, 0, 0) + dot_of(own_ref[...], rows_low, 0, 0)) * (1.0 / tokens)
+
+
+def iterate(joint_all, basis_all, own_rows):
+    tokens, joint = joint_all.shape
+    rank = basis_all.shape[1]
+    return pl.pallas_call(
+        iterate_kernel,
+        out_shape=jax.ShapeDtypeStruct((own_rows.shape[1], rank), jnp.float32),
+        in_specs=[pl.BlockSpec(memory_space=pltpu.VMEM)] * 3,
+        out_specs=pl.BlockSpec(memory_space=pltpu.VMEM),
+        scratch_shapes=[
+            pltpu.VMEM((tokens, tokens), jnp.bfloat16),
+            pltpu.VMEM((tokens, tokens), jnp.bfloat16),
+            pltpu.VMEM((tokens, rank), jnp.float32),
+            pltpu.VMEM((tokens, rank), jnp.float32),
+            pltpu.VMEM((rank, rank), jnp.float32),
+            pltpu.VMEM((LANES, LANES), jnp.float32),
+        ],
+        compiler_params=pltpu.CompilerParams(vmem_limit_bytes=60 * 2**20),
+    )(joint_all, basis_all, own_rows)
+
+
 def body(hidden, gain, key_weight, value_weight, positions, initial_basis):
     hidden_rows = hidden[0]
     local_tokens = positions.shape[1]
@@ -80,6 +227,11 @@
     joint_rows = (
         jnp.stack([key_rows, value_rows], axis=2).reshape(local_tokens, -1).astype(jnp.bfloat16)
     )
+    tokens = local_tokens * lax.axis_size("seq") * lax.axis_size("batch")
+    if tokens <= initial_basis.shape[0] * lax.axis_size("head"):
+        own_rows = lax.all_gather(joint_rows, ("batch", "seq"), axis=0, tiled=True)
+        joint_all = lax.all_gather(own_rows, "head", axis=1, tiled=True)
+        return iterate(joint_all, whole_of(initial_basis), own_rows)
     partial_value = lax.dot_general(
         joint_rows,
         lax.all_gather(joint_rows, "head", axis=1, tiled=True),

time: 719 us -> 310 us (0.43)
  the two profiles are of different devices: /device:TPU:0 before, /device:TPU:9 now
where the time goes in v1:
time: 310 us; the launch traced here: 306 us
  waiting for transfers between devices  158 us (51%)
  Pallas kernels  118 us (38%)
  between operations  13.2 us (4%)
  matrix products  7.8 us (3%)
  other arithmetic  4.69 us (2%)
  blocking collectives  3.77 us (1%)
    pallas_call x1, Pallas kernels, iterate(): pl.pallas_call(iterate_kernel, out_shape=jax.ShapeDtypeStruct((own_rows.s...  118 us
    all_gather x1, waiting for transfers between devices, body(): joint_all = lax.all_gather(own_rows, 'head', axis=1, tiled=True)  80.2 us
    all_gather x1, waiting for transfers between devices, whole_of(): return lax.all_gather(basis_block, 'head', axis=0, tiled=True)  45 us
    all_gather x1, waiting for transfers between devices, body(): own_rows = lax.all_gather(joint_rows, ('batch', 'seq'), axis=0, tiled=True)  23.2 us
    reduce_scatter x1, waiting for transfers between devices, body(): lax.psum_scatter(jnp.dot(scaled, weights, preferred_element_type=jnp.floa...  8.51 us
    dot_general x1, matrix products, body(): jnp.dot(scaled, weights, preferred_element_type=jnp.float32)  7.8 us
  transfers between devices with their start and end apart: 4, of which 4 were waited for; matrix products, arithmetic and copies ran while one was open for 1% of the time, Pallas kernels for 0%

profile of v1, /device:TPU:9, one launch (start us, length us, event | category | flops | bytes accessed | tf_op | source)
XLA Modules:
  0.0 306.0 jit_solution(13733057412811293142)
XLA Ops:
  6.5 0.0 reduce-scatter.2.cloned.1.call-start
  6.5 7.8 %fusion.2 = f32[256,512]{1,0:T(8,128)} fusion(bf16[8192,256]{1,0:T(8,128)(2,1)} %param.9, bf16[8192,256]{1,0:T(8,128)(2,1)} %param.8, bf16[1,256,8192]{2,1,0:T(8,128)(2,1)} %param.6, f32[8192]{0:T(1024)} %param.7), kind=kOutput, calls=%fused_computation.4 | convolution fusion | flops 2170552320 | bytes 13139968 | tf_op jit(solution)/shard_map/dot_general | solution.py:218
  14.3 0.0 copy-start
  14.3 0.0 reduce-scatter.2.cloned.1.call-update
  14.4 0.0 all-gather.4.cloned.1.call-start
  14.4 3.1 %fusion.1 = f32[256]{0:T(256)S(1)} fusion(bf16[1,256,8192]{2,1,0:T(8,128)(2,1)} %param.6), kind=kLoop, calls=%fused_computation.3 | loop fusion | flops 6291200 | bytes 4195328 | tf_op jit(solution)/shard_map/reduce_sum | solution.py:213
  17.5 3.8 %psum.7 = f32[256]{0:T(256)S(1)} all-reduce(f32[256]{0:T(256)S(1)} %fusion.1), channel_id=1, replica_groups=mesh['seq'=2,'batch'=4,'head'=4] {'seq'}, use_global_device_ids=true, to_apply=%region_2.0 | all-reduce | flops 256 | bytes 2048 | tf_op jit(solution)/shard_map/psum | solution.py:42
  21.3 0.1 add_rsqrt_fusion
  21.4 0.0 copy-done
  21.4 0.3 multiply_cosine_fusion
  21.7 8.5 %reduce-scatter.2.cloned.1.call-done = f32[128,512]{1,0:T(8,128)} async-done(((f32[256,512]{1,0:T(8,128)}), f32[128,512]{1,0:T(8,128)}) %reduce-scatter.2.cloned.1.call-update) | async-done | bytes 262160 | tf_op jit(solution)/shard_map/reduce_scatter | solution.py:217
  30.2 1.0 broadcast_multiply_fusion
  31.3 0.1 reshape.67
  31.4 0.2 fusion.10
  31.7 0.1 maximum_bitcast_fusion
  31.8 0.1 copy.11
  31.9 0.7 convert_element_type.28
  32.7 0.0 all-gather.4.cloned.1.call-update
  32.7 0.0 all-gather.8.cloned.1.call-start
  32.7 0.7 all-gather.8.cloned.1.call-update
  33.4 0.0 all-gather.6.cloned.1.call-start
  33.5 23.2 %all-gather.4.cloned.1.call-done.own_ref = bf16[1024,512]{1,0:T(8,128)(2,1)} async-done(((bf16[128,512]{1,0:T(8,128)(2,1)}), bf16[1024,512]{1,0:T(8,128)(2,1)}) %all-gather.4.cloned.1.call-update) | async-done | bytes 1048592 | tf_op jit(solution)/shard_map/all_gather | solution.py:232
  56.7 0.0 all-gather.6.cloned.1.call-update
  56.7 45.0 %all-gather.8.cloned.1.call-done.basis_ref = f32[2048,256]{1,0:T(8,128)} async-done(((f32[512,256]{1,0:T(8,128)}), f32[2048,256]{1,0:T(8,128)}) %all-gather.8.cloned.1.call-update) | async-done | bytes 2097168 | tf_op jit(solution)/shard_map/all_gather | solution.py:38
  101.7 80.2 %all-gather.6.cloned.1.call-done.joint_ref = bf16[1024,2048]{1,0:T(8,128)(2,1)} async-done(((bf16[1024,512]{1,0:T(8,128)(2,1)}), bf16[1024,2048]{1,0:T(8,128)(2,1)}) %all-gather.6.cloned.1.call-update) | async-done | bytes 4194320 | tf_op jit(solution)/shard_map/all_gather | solution.py:233
  181.9 117.6 %shard_map.64 = f32[512,256]{1,0:T(8,128)} custom-call(bf16[1024,2048]{1,0:T(8,128)(2,1)} %all-gather.6.cloned.1.call-done.joint_ref, f32[2048,256]{1,0:T(8,128)} %all-gather.8.cloned.1.call-done.basis_ref, bf16[1024,512]{1,0:T(8,128)(2,1)} %all-gather.4.cloned.1.call-done.own_ref), custom_call_target="tpu_custom_call" | custom-call | tf_op jit(solution)/shard_map/pallas_call | solution.py:191
  (8 shorter events, 0.1 us)
Async XLA Ops:
  6.5 23.7 %reduce-scatter.2.cloned.1.call-start = ((), (), s32[]{:S(2)}) async-start(), calls=%async_computation.1 | async-start | bytes 786432 | tf_op jit(solution)/shard_map/reduce_scatter | solution.py:217
  14.3 7.0 %copy-start = (s32[1,128]{1,0:T(1,128)S(1)}, s32[1,128]{1,0:T(1,128)}, u32[]{:S(2)}) copy-start(s32[1,128]{1,0:T(1,128)} %param.10) | copy-start | bytes 1540
  14.4 42.3 %all-gather.4.cloned.1.call-start = ((), (), s32[]{:S(2)}) async-start(), calls=%async_computation.2 | async-start | bytes 1179648 | tf_op jit(solution)/shard_map/all_gather | solution.py:232
  32.7 69.1 %all-gather.8.cloned.1.call-start = ((), (), s32[]{:S(2)}) async-start(), calls=%async_computation.4 | async-start | bytes 2621440 | tf_op jit(solution)/shard_map/all_gather | solution.py:38
  33.4 148.5 %all-gather.6.cloned.1.call-start = ((), (), s32[]{:S(2)}) async-start(), calls=%async_computation.3 | async-start | bytes 5242880 | tf_op jit(solution)/shard_map/all_gather | solution.py:233
Sparse Core Ops, SparseCore 0:
  14.5 15.6 reduce-scatter.1
  32.8 23.8 all-gather.3
  58.3 43.4 all-gather.7
  103.2 78.7 all-gather.5

commit v2 on v1

--- a/solution.py
+++ b/solution.py
@@ -1,3 +1,4 @@
+import functools
 import math
 
 import jax
@@ -139,7 +140,9 @@
     return jnp.concatenate(blocks, axis=0)
 
 
-def iterate_kernel(joint_ref, basis_ref, own_ref, out_ref, high_ref, low_ref, rows_ref, images_ref, gram_ref, inverse_ref):
+def iterate_kernel(
+    joint_ref, basis_ref, out_ref, high_ref, low_ref, rows_ref, images_ref, gram_ref
+):
     tokens, joint = joint_ref.shape
     rank = basis_ref.shape[1]
     panels = rank // LANES
@@ -182,16 +185,18 @@
 
     lax.fori_loop(0, ITERS, step, 0)
     rows_high, rows_low = halves_of(rows_ref[...])
-    out_ref[...] = (dot_of(own_ref[...], rows_high, 0, 0) + dot_of(own_ref[...], rows_low, 0, 0)) * (1.0 / tokens)
-
-
-def iterate(joint_all, basis_all, own_rows):
+    width = out_ref.shape[0]
+    own = joint_ref[:, pl.ds(pl.multiple_of(lax.axis_index("head") * width, width), width)]
+    out_ref[...] = (dot_of(own, rows_high, 0, 0) + dot_of(own, rows_low, 0, 0)) * (1.0 / tokens)
+
+
+def iterate(joint_all, basis_all):
     tokens, joint = joint_all.shape
     rank = basis_all.shape[1]
     return pl.pallas_call(
         iterate_kernel,
-        out_shape=jax.ShapeDtypeStruct((own_rows.shape[1], rank), jnp.float32),
-        in_specs=[pl.BlockSpec(memory_space=pltpu.VMEM)] * 3,
+        out_shape=jax.ShapeDtypeStruct((joint // lax.axis_size("head"), rank), jnp.float32),
+        in_specs=[pl.BlockSpec(memory_space=pltpu.VMEM)] * 2,
         out_specs=pl.BlockSpec(memory_space=pltpu.VMEM),
         scratch_shapes=[
             pltpu.VMEM((tokens, tokens), jnp.bfloat16),
@@ -199,15 +204,229 @@
             pltpu.VMEM((tokens, rank), jnp.float32),
             pltpu.VMEM((tokens, rank), jnp.float32),
             pltpu.VMEM((rank, rank), jnp.float32),
-            pltpu.VMEM((LANES, LANES), jnp.float32),
         ],
-        compiler_params=pltpu.CompilerParams(vmem_limit_bytes=60 * 2**20),
-    )(joint_all, basis_all, own_rows)
+        compiler_params=pltpu.CompilerParams(vmem_limit_bytes=40 * 2**20),
+    )(joint_all, basis_all)
+
+
+def project_kernel(hidden_ref, gain_ref, key_ref, value_ref, partial_ref, squares_ref):
+    key_columns = key_ref.shape[1]
+
+    @pl.when(pl.program_id(0) == 0)
+    def _():
+        partial_ref[...] = jnp.zeros_like(partial_ref)
+        squares_ref[...] = jnp.zeros_like(squares_ref)
+
+    widened = hidden_ref[...].astype(jnp.float32)
+    scaled = (widened * gain_ref[...]).astype(jnp.bfloat16)
+    partial_ref[:, :key_columns] += dot_of(scaled, key_ref[...], 1, 0)
+    partial_ref[:, key_columns:] += dot_of(scaled, value_ref[...], 1, 0)
+    squared = widened * widened
+    total = squares_ref[...]
+    for start in range(0, squared.shape[1], LANES):
+        total = total + squared[:, start : start + LANES]
+    squares_ref[...] = total
+
+
+def project(hidden_rows, gain, key_weight, value_weight):
+    tokens, depth = hidden_rows.shape
+    key_columns, value_columns = key_weight.shape[1], value_weight.shape[1]
+    chunk = math.gcd(depth, 1024)
+    return pl.pallas_call(
+        project_kernel,
+        grid=(depth // chunk,),
+        out_shape=(
+            jax.ShapeDtypeStruct((tokens, key_columns + value_columns), jnp.float32),
+            jax.ShapeDtypeStruct((tokens, LANES), jnp.float32),
+        ),
+        in_specs=[
+            pl.BlockSpec((tokens, chunk), lambda step: (0, step)),
+            pl.BlockSpec((1, chunk), lambda step: (0, step)),
+            pl.BlockSpec((chunk, key_columns), lambda step: (step, 0)),
+            pl.BlockSpec((chunk, value_columns), lambda step: (step, 0)),
+        ],
+        out_specs=(
+            pl.BlockSpec((tokens, key_columns + value_columns), lambda step: (0, 0)),
+            pl.BlockSpec((tokens, LANES), lambda step: (0, 0)),
+        ),
+        compiler_params=pltpu.CompilerParams(
+            dimension_semantics=("arbitrary",), vmem_limit_bytes=60 * 2**20
+        ),
+    )(hidden_rows, gain[None, :], key_weight, value_weight)
+
+
+def gather_kernel(
+    heads,
+    partial_ref,
+    squares_ref,
+    cosine_ref,
+    sine_ref,
+    out_ref,
+    peer_partial,
+    peer_squares,
+    swap_sems,
+    z_sems,
+    x_sems,
+    y_sems,
+    x_half_sems,
+    y_half_sems,
+    core_sems,
+):
+    x, b, z = lax.axis_index("seq"), lax.axis_index("batch"), lax.axis_index("head")
+    local, width = peer_partial.shape
+    half = width // 2
+    other_x, other_y = 1 - x, (b + 2) % 4
+    partner = b + 1 - 2 * (b % 2)
+    x_peer, y_peer, core_peer = (other_x, b, z), (x, other_y, z), (x, partner, z)
+
+    def z_peer(d):
+        return (x, b, (z + d) % heads)
+
+    barrier = pltpu.get_barrier_semaphore()
+    peers = [x_peer, y_peer, core_peer] + [z_peer(d) for d in range(1, heads)]
+    for peer in peers:
+        pl.semaphore_signal(barrier, inc=1, device_id=peer, device_id_type=pl.DeviceIdType.MESH)
+    pl.semaphore_wait(barrier, len(peers))
+
+    def copy(source, target, sems, peer):
+        return pltpu.make_async_remote_copy(
+            src_ref=source,
+            dst_ref=target,
+            send_sem=sems.at[0],
+            recv_sem=sems.at[1],
+            device_id=peer,
+            device_id_type=pl.DeviceIdType.MESH,
+        )
+
+    def region(xs, bs, zs, start=0, size=width):
+        row = pl.multiple_of((xs * 4 + bs) * local, local)
+        column = pl.multiple_of(zs * width + start, half)
+        return out_ref.at[pl.ds(row, local), pl.ds(column, size)]
+
+    started = []
+
+    def send(area, sems, peer):
+        going = copy(area, area, sems, peer)
+        going.start()
+        started.append(going)
+
+    def arrive(area, sems, peer):
+        copy(area, area, sems, peer).wait_recv()
+
+    away = pl.ds(pl.multiple_of(other_x * local, local), local)
+    mine = pl.ds(pl.multiple_of(x * local, local), local)
+    swaps = [
+        copy(partial_ref.at[away, :], peer_partial, swap_sems.at[0], x_peer),
+        copy(squares_ref.at[away, :], peer_squares, swap_sems.at[1], x_peer),
+    ]
+    for swap in swaps:
+        swap.start()
+    for swap in swaps:
+        swap.wait()
+    squares = jnp.sum(squares_ref[mine, :] + peer_squares[...], axis=1, keepdims=True)
+    projected = (partial_ref[mine, :] + peer_partial[...]) * lax.rsqrt(squares / D + EPSILON)
+    row = pl.multiple_of((x * 4 + b) * local, local)
+    for g in range(half // HEAD_DIM):
+        key = projected[:, g * HEAD_DIM : (g + 1) * HEAD_DIM]
+        turned = key * cosine_ref[...] + pltpu.roll(key, HEAD_DIM // 2, 1) * sine_ref[...]
+        value = projected[:, half + g * HEAD_DIM : half + (g + 1) * HEAD_DIM]
+        column = pl.multiple_of(z * width + 2 * g * HEAD_DIM, HEAD_DIM)
+        out_ref[pl.ds(row, local), pl.ds(column, HEAD_DIM)] = turned.astype(jnp.bfloat16)
+        column = pl.multiple_of(z * width + (2 * g + 1) * HEAD_DIM, HEAD_DIM)
+        out_ref[pl.ds(row, local), pl.ds(column, HEAD_DIM)] = value.astype(jnp.bfloat16)
+
+    for d in range(1, heads):
+        send(region(x, b, z), z_sems.at[d], z_peer(d))
+
+    def source(d):
+        return (z + heads - d) % heads
+
+    def spread(d):
+        area = region(x, b, source(d))
+        if d:
+            arrive(area, z_sems.at[d], z_peer(d))
+        send(area, x_sems.at[d], x_peer)
+        send(area, y_sems.at[d], y_peer)
+        send(area, core_sems.at[d, 0], core_peer)
+
+    def relay(d):
+        s = source(d)
+        arrive(region(other_x, b, s), x_sems.at[d], x_peer)
+        send(region(other_x, b, s, half, half), y_half_sems.at[d], y_peer)
+        send(region(other_x, b, s), core_sems.at[d, 1], core_peer)
+        arrive(region(x, other_y, s), y_sems.at[d], y_peer)
+        send(region(x, other_y, s, 0, half), x_half_sems.at[d], x_peer)
+        send(region(x, other_y, s), core_sems.at[d, 2], core_peer)
+
+    def finish(d):
+        s = source(d)
+        arrive(region(other_x, other_y, s, 0, half), x_half_sems.at[d], x_peer)
+        arrive(region(other_x, other_y, s, half, half), y_half_sems.at[d], y_peer)
+        send(region(other_x, other_y, s), core_sems.at[d, 3], core_peer)
+
+    order = [0] + sorted(range(1, heads), key=lambda d: (min(d, heads - d), d))
+    for turn in range(heads + 2):
+        if turn < heads:
+            spread(order[turn])
+        if 1 <= turn < heads + 1:
+            relay(order[turn - 1])
+        if turn >= 2:
+            finish(order[turn - 2])
+    far = (partner + 2) % 4
+    for d in order:
+        s = source(d)
+        areas = [(x, partner), (other_x, partner), (x, far), (other_x, far)]
+        for kind, (xs, bs) in enumerate(areas):
+            arrive(region(xs, bs, s), core_sems.at[d, kind], core_peer)
+    for going in started:
+        going.wait_send()
+
+
+def gather(partial, squares, positions, heads, tokens):
+    local, width = positions.shape[0], partial.shape[1]
+    half_width = HEAD_DIM // 2
+    frequency = jnp.exp(
+        jnp.arange(half_width, dtype=jnp.float32) * (-math.log(ROTARY_BASE) / half_width)
+    )
+    angles = positions.astype(jnp.float32)[:, None] * frequency[None, :]
+    cosine, sine = jnp.cos(angles), jnp.sin(angles)
+    dma = pltpu.SemaphoreType.DMA
+    return pl.pallas_call(
+        functools.partial(gather_kernel, heads),
+        out_shape=jax.ShapeDtypeStruct((tokens, heads * width), jnp.bfloat16),
+        in_specs=[pl.BlockSpec(memory_space=pltpu.VMEM)] * 4,
+        out_specs=pl.BlockSpec(memory_space=pltpu.VMEM),
+        scratch_shapes=[
+            pltpu.VMEM((local, width), jnp.float32),
+            pltpu.VMEM((local, LANES), jnp.float32),
+            dma((2, 2)),
+            dma((heads, 2)),
+            dma((heads, 2)),
+            dma((heads, 2)),
+            dma((heads, 2)),
+            dma((heads, 2)),
+            dma((heads, 4, 2)),
+        ],
+        compiler_params=pltpu.CompilerParams(
+            collective_id=0, has_side_effects=True, vmem_limit_bytes=24 * 2**20
+        ),
+    )(
+        partial,
+        squares,
+        jnp.concatenate([cosine, cosine], axis=1),
+        jnp.concatenate([-sine, sine], axis=1),
+    )
 
 
 def body(hidden, gain, key_weight, value_weight, positions, initial_basis):
     hidden_rows = hidden[0]
     local_tokens = positions.shape[1]
+    seqs, batches, heads = lax.axis_size("seq"), lax.axis_size("batch"), lax.axis_size("head")
+    tokens = local_tokens * seqs * batches
+    if seqs == 2 and batches == 4 and tokens <= initial_basis.shape[0] * heads:
+        partial, squares = project(hidden_rows, gain, key_weight, value_weight)
+        joint_all = gather(partial, squares, positions[0], heads, tokens)
+        return iterate(joint_all, whole_of(initial_basis))
     widened = hidden_rows.astype(jnp.float32)
     scaled = (widened * gain).astype(jnp.bfloat16)
     local_squares = jnp.sum(widened * widened, axis=1)
@@ -227,11 +446,6 @@
     joint_rows = (
         jnp.stack([key_rows, value_rows], axis=2).reshape(local_tokens, -1).astype(jnp.bfloat16)
     )
-    tokens = local_tokens * lax.axis_size("seq") * lax.axis_size("batch")
-    if tokens <= initial_basis.shape[0] * lax.axis_size("head"):
-        own_rows = lax.all_gather(joint_rows, ("batch", "seq"), axis=0, tiled=True)
-        joint_all = lax.all_gather(own_rows, "head", axis=1, tiled=True)
-        return iterate(joint_all, whole_of(initial_basis), own_rows)
     partial_value = lax.dot_general(
         joint_rows,
         lax.all_gather(joint_rows, "head", axis=1, tiled=True),

time: 310 us -> 200 us (0.65); the launches traced: 306 us -> 199 us
  waiting for transfers between devices: 158 us -> 0.71 us
  Pallas kernels: 118 us -> 177 us
  matrix products: 7.8 us -> 0 us
  local copies, waits for them, and re-layouts: 1.18 us -> 7.72 us
  other arithmetic: 4.69 us -> 0.42 us
  blocking collectives: 3.77 us -> 0 us
    all_gather x2 -> x0, waiting for transfers between devices: 103 us -> none  [the longest x1 80.2 us: body(): joint_all = lax.all_gather(own_rows, 'head', axis=1, tiled=True)]
    pallas_call x1 -> x3, Pallas kernels: 118 us -> 177 us  [the longest x1 115 us: iterate(): pl.pallas_call(iterate_kernel, out_shape=jax.ShapeDtypeStruct((joint // l...]
    all_gather x1, waiting for transfers between devices: 45 us -> 0.01 us  [whole_of(): return lax.all_gather(basis_block, 'head', axis=0, tiled=True)]
    reduce_scatter x1 -> x0, waiting for transfers between devices: 8.51 us -> none  [body(): lax.psum_scatter(jnp.dot(scaled, weights, preferred_element_type=jnp.floa...]
    dot_general x1 -> x0, matrix products: 7.8 us -> none  [body(): jnp.dot(scaled, weights, preferred_element_type=jnp.float32)]
    unnamed x2 -> x12, local copies, waits for them, and re-layouts: 0.01 us -> 7.72 us
    psum x1 -> x0, blocking collectives: 3.77 us -> none  [total_squares(): all_squares = lax.psum(local_squares, 'seq')]
    reduce_sum x1 -> x0, other arithmetic: 3.1 us -> none  [body(): local_squares = jnp.sum(widened * widened, axis=1)]
  transfers between devices with their start and end apart: 4 -> 1, of which waited for: 4 -> 0; matrix products, arithmetic and copies ran while one was open for 1% -> 0% of each run, Pallas kernels for 0% -> 31%
where the time goes in v2:
time: 200 us; the launch traced here: 199 us
  Pallas kernels  177 us (88%)
  between operations  13.5 us (7%)
  local copies, waits for them, and re-layouts  7.72 us (4%)
    pallas_call x1, Pallas kernels, iterate(): pl.pallas_call(iterate_kernel, out_shape=jax.ShapeDtypeStruct((joint // l...  115 us
    pallas_call x1, Pallas kernels, gather(): pl.pallas_call(functools.partial(gather_kernel, heads), out_shape=jax.Sha...  53.5 us
    pallas_call x1, Pallas kernels, project(): pl.pallas_call(project_kernel, grid=(depth // chunk,), out_shape=(jax.Sha...  9.02 us
    unnamed x12, local copies, waits for them, and re-layouts  7.72 us
  transfers between devices with their start and end apart: 1, of which 0 were waited for; matrix products, arithmetic and copies ran while one was open for 0% of the time, Pallas kernels for 31%

profile of v2, /device:TPU:9, one launch (start us, length us, event | category | flops | bytes accessed | tf_op | source)
XLA Modules:
  0.0 199.3 jit_solution(6413996015805102999)
XLA Ops:
  6.5 0.0 all-gather.2.cloned.1.call-start
  6.5 0.7 all-gather.2.cloned.1.call-update
  7.3 0.0 copy-start.5
  7.3 9.0 %shard_map.64 = (f32[256,512]{1,0:T(8,128)}, f32[256,128]{1,0:T(8,128)}) custom-call(bf16[256,8192]{1,0:T(8,128)(2,1)} %bitcast.4, f32[1,8192]{1,0:T(1,128)} %bitcast.5, bf16[8192,256]{1,0:T(8,128)(2,1)} %key_ref.1, bf16[8192,256]{1,0:T(8,128)(2,1)} %value_ref.1), custom_call_target="tpu_custom_call" | custom-call | tf_op jit(solution)/shard_map/pallas_call | solution.py:235
  16.3 0.0 copy-done.5
  16.3 0.3 fusion
  16.6 0.1 pad_maximum_fusion
  16.7 0.0 copy-start.3
  16.8 1.1 copy-done.3
  17.8 0.0 copy-start.4
  17.8 0.9 copy-done.4
  18.7 53.5 %shard_map.65.joint_ref = bf16[1024,2048]{1,0:T(8,128)(2,1)S(1)} custom-call(f32[256,512]{1,0:T(8,128)S(1)} %copy-done.3, f32[256,128]{1,0:T(8,128)S(1)} %copy-done.4, f32[128,128]{1,0:T(8,128)S(1)} %get-tuple-element.12.cosine_ref, f32[128,128]{1,0:T(8,128)S(1)} %get-tuple-element.13.sine_ref), custom_call_target="tpu_custom_call" | custom-call | tf_op jit(solution)/shard_map/pallas_call | solution.py:394
  72.2 0.0 copy-start
  72.2 1.9 copy-done
  74.2 0.0 all-gather.2.cloned.1.call-done.basis_ref
  74.2 0.0 copy-start.1
  74.2 2.2 %copy-done.1 = bf16[1024,2048]{1,0:T(8,128)(2,1)S(1)} copy-done((bf16[1024,2048]{1,0:T(8,128)(2,1)S(1)}, bf16[1024,2048]{1,0:T(8,128)(2,1)}, u32[]{:S(2)}) %copy-start.1) | copy-done | bytes 4194328
  76.4 0.0 copy-start.2
  76.4 1.6 copy-done.2
  78.0 114.5 %shard_map.66 = f32[512,256]{1,0:T(8,128)} custom-call(bf16[1024,2048]{1,0:T(8,128)(2,1)S(1)} %copy-done.1, f32[2048,256]{1,0:T(8,128)S(1)} %copy-done.2), custom_call_target="tpu_custom_call" | custom-call | tf_op jit(solution)/shard_map/pallas_call | solution.py:196
  (2 shorter events, 0.0 us)
Async XLA Ops:
  6.5 67.6 %all-gather.2.cloned.1.call-start = ((), (), s32[]{:S(2)}) async-start(), calls=%async_computation | async-start | bytes 2621440 | tf_op jit(solution)/shard_map/all_gather | solution.py:39
  7.3 9.0 %copy-start.5 = (s32[1,128]{1,0:T(1,128)S(1)}, s32[1,128]{1,0:T(1,128)}, u32[]{:S(2)}) copy-start(s32[1,128]{1,0:T(1,128)} %param.10) | copy-start | bytes 1540
  16.7 1.1 copy-start.3
  17.8 0.9 copy-start.4
  72.2 2.0 copy-start
  74.2 2.2 %copy-start.1 = (bf16[1024,2048]{1,0:T(8,128)(2,1)S(1)}, bf16[1024,2048]{1,0:T(8,128)(2,1)}, u32[]{:S(2)}) copy-start(bf16[1024,2048]{1,0:T(8,128)(2,1)} %copy-done) | copy-start | bytes 12582916
  76.4 1.6 copy-start.2
Sparse Core Ops, SparseCore 0:
  8.9 54.8 all-gather.1

commit v3 on v2

--- a/solution.py
+++ b/solution.py
@@ -84,6 +84,43 @@
     return high, (value - high.astype(jnp.float32)).astype(jnp.bfloat16)
 
 
+def small_inverse(block):
+    size = len(block)
+    block = [list(line) for line in block]
+    extra = [[None] * size for _ in range(size)]
+    result = [[None] * size for _ in range(size)]
+
+    def plus(left, right):
+        return right if left is None else left if right is None else left + right
+
+    def times(scale, value):
+        return None if value is None else scale if isinstance(value, float) else scale * value
+
+    def minus(left, right):
+        return left if right is None else -right if left is None else left - right
+
+    for i in range(size):
+        extra[i][i] = 1.0
+    for k in range(0, size, 2):
+        first, cross, last = block[k][k], block[k + 1][k], block[k + 1][k + 1]
+        scale = 1.0 / (first * last - cross * cross)
+        for i in range(k + 2, size):
+            one, two = block[i][k], block[i][k + 1]
+            top = (one * last - two * cross) * scale
+            low = (two * first - one * cross) * scale
+            for j in range(k + 2, i + 1):
+                block[i][j] = block[i][j] - (top * block[j][k] + low * block[j][k + 1])
+            for j in range(k + 2):
+                change = plus(times(top, extra[k][j]), times(low, extra[k + 1][j]))
+                extra[i][j] = minus(extra[i][j], change)
+        ratio = cross / first
+        top_scale, low_scale = lax.rsqrt(first), lax.rsqrt(last - ratio * cross)
+        for j in range(k + 2):
+            result[k][j] = times(top_scale, extra[k][j])
+            result[k + 1][j] = times(low_scale, minus(extra[k + 1][j], times(ratio, extra[k][j])))
+    return result
+
+
 def inverse_factor(matrix):
     size = matrix.shape[0]
     rows = lax.broadcasted_iota(jnp.int32, (SUBLANES, size), 0)
@@ -91,7 +128,6 @@
     groups = size // SUBLANES
     left = [matrix[SUBLANES * g : SUBLANES * (g + 1)] for g in range(groups)]
     right = [jnp.where(lanes == rows + SUBLANES * g, 1.0, 0.0) for g in range(groups)]
-    done = []
 
     def spread_row(value, at):
         return jnp.broadcast_to(value[at : at + 1, :], (SUBLANES, size))
@@ -99,45 +135,40 @@
     def spread_lane(value, at):
         return jnp.broadcast_to(value[:, at : at + 1], (SUBLANES, size))
 
-    for pivot in range(0, size, 2):
-        own, at = pivot // SUBLANES, pivot % SUBLANES
-        top, low = spread_row(left[own], at), spread_row(left[own], at + 1)
-        top_right, low_right = spread_row(right[own], at), spread_row(right[own], at + 1)
-        first, cross, last = (
-            spread_lane(top, pivot),
-            spread_lane(top, pivot + 1),
-            spread_lane(low, pivot + 1),
-        )
-        scale = 1.0 / (first * last - cross * cross)
-        mix_top = (top * last - low * cross) * scale
-        mix_low = (low * first - top * cross) * scale
-        mix_top_right = (top_right * last - low_right * cross) * scale
-        mix_low_right = (low_right * first - top_right * cross) * scale
-        ratio = cross / first
-        done.append(
-            (
-                top_right * lax.rsqrt(first),
-                (low_right - ratio * top_right) * lax.rsqrt(last - ratio * cross),
-            )
-        )
-        for g in range(own, groups):
-            if g == own and at + 2 >= SUBLANES:
-                continue
-            one, two = spread_lane(left[g], pivot), spread_lane(left[g], pivot + 1)
-            if g == own:
-                one = jnp.where(rows > at + 1, one, 0.0)
-                two = jnp.where(rows > at + 1, two, 0.0)
-            left[g] = left[g] - one * mix_top - two * mix_low
-            right[g] = right[g] - one * mix_top_right - two * mix_low_right
-    blocks = []
-    for g in range(groups):
-        block = jnp.zeros((SUBLANES, size), jnp.float32)
-        for pair in range(SUBLANES // 2):
-            upper, lower = done[g * SUBLANES // 2 + pair]
-            block = jnp.where(rows == 2 * pair, upper, block)
-            block = jnp.where(rows == 2 * pair + 1, lower, block)
-        blocks.append(block)
-    return jnp.concatenate(blocks, axis=0)
+    def stacked(values):
+        total = jnp.zeros((SUBLANES, size), jnp.float32)
+        for i, value in enumerate(values):
+            if value is not None:
+                total = jnp.where(rows == i, value, total)
+        return total
+
+    def combined(columns, value):
+        terms = [columns[j] * spread_row(value, j) for j in range(SUBLANES)]
+        while len(terms) > 1:
+            terms = [terms[i] + terms[i + 1] for i in range(0, len(terms), 2)]
+        return terms[0]
+
+    for own in range(groups):
+        pivot = own * SUBLANES
+        tops = [spread_row(left[own], i) for i in range(SUBLANES)]
+        block = [[spread_lane(tops[i], pivot + j) for j in range(i + 1)] for i in range(SUBLANES)]
+        small = small_inverse(block)
+        down = [stacked([small[i][j] for i in range(SUBLANES)]) for j in range(SUBLANES)]
+        across = [stacked([small[j][i] for i in range(SUBLANES)]) for j in range(SUBLANES)]
+        scaled_left, scaled_right = combined(down, left[own]), combined(down, right[own])
+        right[own] = scaled_right
+        if own + 1 == groups:
+            break
+        mixed_left, mixed_right = combined(across, scaled_left), combined(across, scaled_right)
+        mixes = [
+            (spread_row(mixed_left, j), spread_row(mixed_right, j)) for j in range(SUBLANES)
+        ]
+        for g in range(own + 1, groups):
+            columns = [spread_lane(left[g], pivot + j) for j in range(SUBLANES)]
+            for j in range(SUBLANES):
+                left[g] = left[g] - columns[j] * mixes[j][0]
+                right[g] = right[g] - columns[j] * mixes[j][1]
+    return jnp.concatenate(right, axis=0)
 
 
 def iterate_kernel(

time: 200 us -> 169 us (0.84)
  Pallas kernels: 177 us -> 146 us
    pallas_call x1, Pallas kernels: 115 us -> 83.9 us  [iterate(): pl.pallas_call(iterate_kernel, out_shape=jax.ShapeDtypeStruct((joint // l...]
  transfers between devices with their start and end apart: 1 -> 1, of which waited for: 0 -> 0; matrix products, arithmetic and copies ran while one was open for 0% -> 0% of each run, Pallas kernels for 31% -> 37%
where the time goes in v3:
time: 169 us
  Pallas kernels  146 us (86%)
  between operations  13.5 us (8%)
  local copies, waits for them, and re-layouts  7.72 us (5%)
    pallas_call x1, Pallas kernels, iterate(): pl.pallas_call(iterate_kernel, out_shape=jax.ShapeDtypeStruct((joint // l...  83.9 us
    pallas_call x1, Pallas kernels, gather(): pl.pallas_call(functools.partial(gather_kernel, heads), out_shape=jax.Sha...  53.5 us
    pallas_call x1, Pallas kernels, project(): pl.pallas_call(project_kernel, grid=(depth // chunk,), out_shape=(jax.Sha...  9.02 us
    unnamed x12, local copies, waits for them, and re-layouts  7.72 us
  transfers between devices with their start and end apart: 1, of which 0 were waited for; matrix products, arithmetic and copies ran while one was open for 0% of the time, Pallas kernels for 37%

profile of v3, /device:TPU:9, one launch (start us, length us, event | category | flops | bytes accessed | tf_op | source)
XLA Modules:
  0.0 168.7 jit_solution(9716775891608799837)
XLA Ops:
  6.5 0.0 all-gather.2.cloned.1.call-start
  6.5 0.7 all-gather.2.cloned.1.call-update
  7.3 0.0 copy-start.5
  7.3 9.0 %shard_map.64 = (f32[256,512]{1,0:T(8,128)}, f32[256,128]{1,0:T(8,128)}) custom-call(bf16[256,8192]{1,0:T(8,128)(2,1)} %bitcast.4, f32[1,8192]{1,0:T(1,128)} %bitcast.5, bf16[8192,256]{1,0:T(8,128)(2,1)} %key_ref.1, bf16[8192,256]{1,0:T(8,128)(2,1)} %value_ref.1), custom_call_target="tpu_custom_call" | custom-call | tf_op jit(solution)/shard_map/pallas_call | solution.py:266
  16.3 0.0 copy-done.5
  16.3 0.3 fusion
  16.6 0.1 pad_maximum_fusion
  16.7 0.0 copy-start.3
  16.8 1.1 copy-done.3
  17.8 0.0 copy-start.4
  17.8 0.9 copy-done.4
  18.7 53.5 %shard_map.65.joint_ref = bf16[1024,2048]{1,0:T(8,128)(2,1)S(1)} custom-call(f32[256,512]{1,0:T(8,128)S(1)} %copy-done.3, f32[256,128]{1,0:T(8,128)S(1)} %copy-done.4, f32[128,128]{1,0:T(8,128)S(1)} %get-tuple-element.12.cosine_ref, f32[128,128]{1,0:T(8,128)S(1)} %get-tuple-element.13.sine_ref), custom_call_target="tpu_custom_call" | custom-call | tf_op jit(solution)/shard_map/pallas_call | solution.py:425
  72.2 0.0 copy-start
  72.2 1.9 %copy-done = bf16[1024,2048]{1,0:T(8,128)(2,1)} copy-done((bf16[1024,2048]{1,0:T(8,128)(2,1)}, bf16[1024,2048]{1,0:T(8,128)(2,1)S(1)}, u32[]{:S(2)}) %copy-start) | copy-done | bytes 4194328
  74.2 0.0 all-gather.2.cloned.1.call-done.basis_ref
  74.2 0.0 copy-start.1
  74.2 2.2 %copy-done.1 = bf16[1024,2048]{1,0:T(8,128)(2,1)S(1)} copy-done((bf16[1024,2048]{1,0:T(8,128)(2,1)S(1)}, bf16[1024,2048]{1,0:T(8,128)(2,1)}, u32[]{:S(2)}) %copy-start.1) | copy-done | bytes 4194328
  76.4 0.0 copy-start.2
  76.4 1.6 copy-done.2
  78.0 83.9 %shard_map.66 = f32[512,256]{1,0:T(8,128)} custom-call(bf16[1024,2048]{1,0:T(8,128)(2,1)S(1)} %copy-done.1, f32[2048,256]{1,0:T(8,128)S(1)} %copy-done.2), custom_call_target="tpu_custom_call" | custom-call | tf_op jit(solution)/shard_map/pallas_call | solution.py:227
  (2 shorter events, 0.0 us)
Async XLA Ops:
  6.5 67.6 %all-gather.2.cloned.1.call-start = ((), (), s32[]{:S(2)}) async-start(), calls=%async_computation | async-start | bytes 2621440 | tf_op jit(solution)/shard_map/all_gather | solution.py:39
  7.3 9.0 %copy-start.5 = (s32[1,128]{1,0:T(1,128)S(1)}, s32[1,128]{1,0:T(1,128)}, u32[]{:S(2)}) copy-start(s32[1,128]{1,0:T(1,128)} %param.10) | copy-start | bytes 1540
  16.7 1.1 copy-start.3
  17.8 0.9 copy-start.4
  72.2 2.0 %copy-start = (bf16[1024,2048]{1,0:T(8,128)(2,1)}, bf16[1024,2048]{1,0:T(8,128)(2,1)S(1)}, u32[]{:S(2)}) copy-start(bf16[1024,2048]{1,0:T(8,128)(2,1)S(1)} %shard_map.65.joint_ref) | copy-start | bytes 12582916
  74.2 2.2 %copy-start.1 = (bf16[1024,2048]{1,0:T(8,128)(2,1)S(1)}, bf16[1024,2048]{1,0:T(8,128)(2,1)}, u32[]{:S(2)}) copy-start(bf16[1024,2048]{1,0:T(8,128)(2,1)} %copy-done) | copy-start | bytes 12582916
  76.4 1.6 copy-start.2
Sparse Core Ops, SparseCore 0:
  8.9 54.8 all-gather.1

commit v4 on v3

--- a/solution.py
+++ b/solution.py
@@ -292,7 +292,9 @@
     squares_ref,
     cosine_ref,
     sine_ref,
+    basis_ref,
     out_ref,
+    whole_ref,
     peer_partial,
     peer_squares,
     swap_sems,
@@ -306,6 +308,8 @@
     x, b, z = lax.axis_index("seq"), lax.axis_index("batch"), lax.axis_index("head")
     local, width = peer_partial.shape
     half = width // 2
+    rank = basis_ref.shape[1]
+    piece = width // 8
     other_x, other_y = 1 - x, (b + 2) % 4
     partner = b + 1 - 2 * (b % 2)
     x_peer, y_peer, core_peer = (other_x, b, z), (x, other_y, z), (x, partner, z)
@@ -334,6 +338,10 @@
         column = pl.multiple_of(zs * width + start, half)
         return out_ref.at[pl.ds(row, local), pl.ds(column, size)]
 
+    def piece_of(xs, bs, zs, start=0, size=rank):
+        row = pl.multiple_of(zs * width + (xs * 4 + bs) * piece, piece)
+        return whole_ref.at[pl.ds(row, piece), pl.ds(start, size)]
+
     started = []
 
     def send(area, sems, peer):
@@ -343,6 +351,16 @@
 
     def arrive(area, sems, peer):
         copy(area, area, sems, peer).wait_recv()
+
+    def source(d):
+        return (z + heads - d) % heads
+
+    order = [0] + sorted(range(1, heads), key=lambda d: (min(d, heads - d), d))
+    own_piece = basis_ref.at[pl.ds(pl.multiple_of((x * 4 + b) * piece, piece), piece), :]
+    for d in range(1, heads):
+        going = copy(own_piece, piece_of(x, b, z), z_sems.at[1, d], z_peer(d))
+        going.start()
+        started.append(going)
 
     away = pl.ds(pl.multiple_of(other_x * local, local), local)
     mine = pl.ds(pl.multiple_of(x * local, local), local)
@@ -352,6 +370,7 @@
     ]
     for swap in swaps:
         swap.start()
+    whole_ref[pl.ds(pl.multiple_of(z * width, width), width), :] = basis_ref[...]
     for swap in swaps:
         swap.wait()
     squares = jnp.sum(squares_ref[mine, :] + peer_squares[...], axis=1, keepdims=True)
@@ -367,53 +386,51 @@
         out_ref[pl.ds(row, local), pl.ds(column, HEAD_DIM)] = value.astype(jnp.bfloat16)
 
     for d in range(1, heads):
-        send(region(x, b, z), z_sems.at[d], z_peer(d))
-
-    def source(d):
-        return (z + heads - d) % heads
-
-    def spread(d):
-        area = region(x, b, source(d))
+        send(region(x, b, z), z_sems.at[0, d], z_peer(d))
+
+    def spread(kind, area, middle, d):
+        mine = area(x, b, source(d))
         if d:
-            arrive(area, z_sems.at[d], z_peer(d))
-        send(area, x_sems.at[d], x_peer)
-        send(area, y_sems.at[d], y_peer)
-        send(area, core_sems.at[d, 0], core_peer)
-
-    def relay(d):
+            arrive(mine, z_sems.at[kind, d], z_peer(d))
+        send(mine, x_sems.at[kind, d], x_peer)
+        send(mine, y_sems.at[kind, d], y_peer)
+        send(mine, core_sems.at[kind, d, 0], core_peer)
+
+    def relay(kind, area, middle, d):
         s = source(d)
-        arrive(region(other_x, b, s), x_sems.at[d], x_peer)
-        send(region(other_x, b, s, half, half), y_half_sems.at[d], y_peer)
-        send(region(other_x, b, s), core_sems.at[d, 1], core_peer)
-        arrive(region(x, other_y, s), y_sems.at[d], y_peer)
-        send(region(x, other_y, s, 0, half), x_half_sems.at[d], x_peer)
-        send(region(x, other_y, s), core_sems.at[d, 2], core_peer)
-
-    def finish(d):
+        arrive(area(other_x, b, s), x_sems.at[kind, d], x_peer)
+        send(area(other_x, b, s, middle, middle), y_half_sems.at[kind, d], y_peer)
+        send(area(other_x, b, s), core_sems.at[kind, d, 1], core_peer)
+        arrive(area(x, other_y, s), y_sems.at[kind, d], y_peer)
+        send(area(x, other_y, s, 0, middle), x_half_sems.at[kind, d], x_peer)
+        send(area(x, other_y, s), core_sems.at[kind, d, 2], core_peer)
+
+    def finish(kind, area, middle, d):
         s = source(d)
-        arrive(region(other_x, other_y, s, 0, half), x_half_sems.at[d], x_peer)
-        arrive(region(other_x, other_y, s, half, half), y_half_sems.at[d], y_peer)
-        send(region(other_x, other_y, s), core_sems.at[d, 3], core_peer)
-
-    order = [0] + sorted(range(1, heads), key=lambda d: (min(d, heads - d), d))
-    for turn in range(heads + 2):
-        if turn < heads:
-            spread(order[turn])
-        if 1 <= turn < heads + 1:
-            relay(order[turn - 1])
+        arrive(area(other_x, other_y, s, 0, middle), x_half_sems.at[kind, d], x_peer)
+        arrive(area(other_x, other_y, s, middle, middle), y_half_sems.at[kind, d], y_peer)
+        send(area(other_x, other_y, s), core_sems.at[kind, d, 3], core_peer)
+
+    joint, pieces = (0, region, half), (1, piece_of, rank // 2)
+    items = [joint + (0,)] + [pieces + (d,) for d in order[1:]] + [joint + (d,) for d in order[1:]]
+    for turn in range(len(items) + 2):
+        if turn < len(items):
+            spread(*items[turn])
+        if 1 <= turn < len(items) + 1:
+            relay(*items[turn - 1])
         if turn >= 2:
-            finish(order[turn - 2])
+            finish(*items[turn - 2])
     far = (partner + 2) % 4
-    for d in order:
+    for kind, area, middle, d in items:
         s = source(d)
-        areas = [(x, partner), (other_x, partner), (x, far), (other_x, far)]
-        for kind, (xs, bs) in enumerate(areas):
-            arrive(region(xs, bs, s), core_sems.at[d, kind], core_peer)
+        places = [(x, partner), (other_x, partner), (x, far), (other_x, far)]
+        for place, (xs, bs) in enumerate(places):
+            arrive(area(xs, bs, s), core_sems.at[kind, d, place], core_peer)
     for going in started:
         going.wait_send()
 
 
-def gather(partial, squares, positions, heads, tokens):
+def gather(partial, squares, positions, basis, heads, tokens):
     local, width = positions.shape[0], partial.shape[1]
     half_width = HEAD_DIM // 2
     frequency = jnp.exp(
@@ -424,19 +441,22 @@
     dma = pltpu.SemaphoreType.DMA
     return pl.pallas_call(
         functools.partial(gather_kernel, heads),
-        out_shape=jax.ShapeDtypeStruct((tokens, heads * width), jnp.bfloat16),
-        in_specs=[pl.BlockSpec(memory_space=pltpu.VMEM)] * 4,
-        out_specs=pl.BlockSpec(memory_space=pltpu.VMEM),
+        out_shape=(
+            jax.ShapeDtypeStruct((tokens, heads * width), jnp.bfloat16),
+            jax.ShapeDtypeStruct((heads * width, basis.shape[1]), jnp.float32),
+        ),
+        in_specs=[pl.BlockSpec(memory_space=pltpu.VMEM)] * 5,
+        out_specs=(pl.BlockSpec(memory_space=pltpu.VMEM),) * 2,
         scratch_shapes=[
             pltpu.VMEM((local, width), jnp.float32),
             pltpu.VMEM((local, LANES), jnp.float32),
             dma((2, 2)),
-            dma((heads, 2)),
-            dma((heads, 2)),
-            dma((heads, 2)),
-            dma((heads, 2)),
-            dma((heads, 2)),
-            dma((heads, 4, 2)),
+            dma((2, heads, 2)),
+            dma((2, heads, 2)),
+            dma((2, heads, 2)),
+            dma((2, heads, 2)),
+            dma((2, heads, 2)),
+            dma((2, heads, 4, 2)),
         ],
         compiler_params=pltpu.CompilerParams(
             collective_id=0, has_side_effects=True, vmem_limit_bytes=24 * 2**20
@@ -446,6 +466,7 @@
         squares,
         jnp.concatenate([cosine, cosine], axis=1),
         jnp.concatenate([-sine, sine], axis=1),
+        basis,
     )
 
 
@@ -456,8 +477,7 @@
     tokens = local_tokens * seqs * batches
     if seqs == 2 and batches == 4 and tokens <= initial_basis.shape[0] * heads:
         partial, squares = project(hidden_rows, gain, key_weight, value_weight)
-        joint_all = gather(partial, squares, positions[0], heads, tokens)
-        return iterate(joint_all, whole_of(initial_basis))
+        return iterate(*gather(partial, squares, positions[0], initial_basis, heads, tokens))
     widened = hidden_rows.astype(jnp.float32)
     scaled = (widened * gain).astype(jnp.bfloat16)
     local_squares = jnp.sum(widened * widened, axis=1)

time: 169 us -> 140 us (0.83); the launches traced: 169 us -> 137 us
  between operations: 13.5 us -> 0.04 us
  Pallas kernels: 146 us -> 134 us
  local copies, waits for them, and re-layouts: 7.72 us -> 1.95 us
    pallas_call x1, Pallas kernels: 53.5 us -> 41.2 us  [gather(): pl.pallas_call(functools.partial(gather_kernel, heads), out_shape=(jax.Sh...]
    unnamed x12 -> x6, local copies, waits for them, and re-layouts: 7.72 us -> 1.95 us
  transfers between devices with their start and end apart: 1 -> 0, of which waited for: 0 -> 0; matrix products, arithmetic and copies ran while one was open for 0% -> 0% of each run, Pallas kernels for 37% -> 0%
where the time goes in v4:
time: 140 us; the launch traced here: 137 us
  Pallas kernels  134 us (96%)
  local copies, waits for them, and re-layouts  1.95 us (1%)
    pallas_call x1, Pallas kernels, iterate(): pl.pallas_call(iterate_kernel, out_shape=jax.ShapeDtypeStruct((joint // l...  83.9 us
    pallas_call x1, Pallas kernels, gather(): pl.pallas_call(functools.partial(gather_kernel, heads), out_shape=(jax.Sh...  41.2 us
    pallas_call x1, Pallas kernels, project(): pl.pallas_call(project_kernel, grid=(depth // chunk,), out_shape=(jax.Sha...  9.08 us

profile of v4, /device:TPU:9, one launch (start us, length us, event | category | flops | bytes accessed | tf_op | source)
XLA Modules:
  0.0 137.2 jit_solution(2477766596687647377)
XLA Ops:
  0.0 0.7 convert_bitcast_fusion
  0.7 0.3 fusion
  1.0 0.1 pad_maximum_fusion
  1.1 0.0 copy-start
  1.1 9.1 %shard_map.64 = (f32[256,512]{1,0:T(8,128)}, f32[256,128]{1,0:T(8,128)}) custom-call(bf16[256,8192]{1,0:T(8,128)(2,1)} %bitcast.4, f32[1,8192]{1,0:T(1,128)} %bitcast.5, bf16[8192,256]{1,0:T(8,128)(2,1)} %key_ref.1, bf16[8192,256]{1,0:T(8,128)(2,1)} %value_ref.1), custom_call_target="tpu_custom_call" | custom-call | tf_op jit(solution)/shard_map/pallas_call | solution.py:266
  10.2 0.0 copy-done
  10.2 0.0 copy-start.1
  10.2 1.0 copy-done.1
  11.2 0.0 copy-start.2
  11.2 0.9 copy-done.2
  12.1 41.2 %shard_map.65 = (bf16[1024,2048]{1,0:T(8,128)(2,1)S(1)}, f32[2048,256]{1,0:T(8,128)S(1)}) custom-call(f32[256,512]{1,0:T(8,128)S(1)} %copy-done.1, f32[256,128]{1,0:T(8,128)S(1)} %copy-done.2, f32[128,128]{1,0:T(8,128)S(1)} %get-tuple-element.16.cosine_ref, f32[128,128]{1,0:T(8,128)S(1)} %get-tuple-element.17.sine_ref, f32[512,256]{1,0:T(8,128)S(1)} %copy-done), custom_call_target="tpu_custom_call" | custom-call | tf_op jit(solution)/shard_map/pallas_call | solution.py:442
  53.4 83.9 %shard_map.66 = f32[512,256]{1,0:T(8,128)} custom-call(bf16[1024,2048]{1,0:T(8,128)(2,1)S(1)} %get-tuple-element.11.joint_ref, f32[2048,256]{1,0:T(8,128)S(1)} %get-tuple-element.12.basis_ref), custom_call_target="tpu_custom_call" | custom-call | tf_op jit(solution)/shard_map/pallas_call | solution.py:227
  (1 shorter events, 0.0 us)
Async XLA Ops:
  1.1 9.1 %copy-start = (f32[512,256]{1,0:T(8,128)S(1)}, f32[512,256]{1,0:T(8,128)}, u32[]{:S(2)}) copy-start(f32[512,256]{1,0:T(8,128)} %basis_ref.1) | copy-start | bytes 1572868
  10.2 1.0 copy-start.1
  11.2 0.9 copy-start.2

commit v5 on v4

--- a/solution.py
+++ b/solution.py
@@ -82,6 +82,16 @@
 def halves_of(value):
     high = value.astype(jnp.bfloat16)
     return high, (value - high.astype(jnp.float32)).astype(jnp.bfloat16)
+
+
+def thrice(left, right, left_axis, right_axis):
+    left_high, left_low = halves_of(left)
+    right_high, right_low = halves_of(right)
+    return (
+        dot_of(left_high, right_high, left_axis, right_axis)
+        + dot_of(left_high, right_low, left_axis, right_axis)
+        + dot_of(left_low, right_high, left_axis, right_axis)
+    )
 
 
 def small_inverse(block):
@@ -172,7 +182,7 @@
 
 
 def iterate_kernel(
-    joint_ref, basis_ref, out_ref, high_ref, low_ref, rows_ref, images_ref, gram_ref
+    joint_ref, basis_ref, out_ref, high_ref, low_ref, rows_ref, gram_ref
 ):
     tokens, joint = joint_ref.shape
     rank = basis_ref.shape[1]
@@ -188,30 +198,31 @@
 
     def step(iteration, carry):
         rows_high, rows_low = halves_of(rows_ref[...])
-        images_ref[...] = (
+        images = (
             dot_of(high_ref[...], rows_high, 1, 0)
             + dot_of(high_ref[...], rows_low, 1, 0)
             + dot_of(low_ref[...], rows_high, 1, 0)
         )
-        gram_ref[...] = exact(rows_ref[...], images_ref[...], 0, 0) * (1.0 / (tokens * joint))
+        images_high, images_low = halves_of(images)
+        gram_ref[...] = (
+            dot_of(rows_high, images_high, 0, 0)
+            + dot_of(rows_high, images_low, 0, 0)
+            + dot_of(rows_low, images_high, 0, 0)
+        ) * (1.0 / (tokens * joint))
 
         @pl.when(iteration < ITERS - 1)
         def _():
-            rows_ref[...] = images_ref[...]
-
-        def panel_step(panel, inner):
-            at = pl.ds(pl.multiple_of(panel * LANES, LANES), LANES)
-            inverse = inverse_factor(gram_ref[at, at])
-            scaled = exact(inverse, gram_ref[at, :], 1, 0)
-            lane = lax.broadcasted_iota(jnp.int32, scaled.shape, 1)
-            scaled = jnp.where(lane >= (panel + 1) * LANES, scaled, 0.0)
-            gram_ref[...] -= exact(scaled, scaled, 0, 0)
-            columns = exact(rows_ref[:, at], inverse, 1, 1)
-            rows_ref[...] -= exact(columns, scaled, 1, 0)
-            rows_ref[:, at] = columns
-            return inner
-
-        lax.fori_loop(0, panels, panel_step, 0)
+            rows_ref[...] = images
+
+        for panel in range(panels):
+            start, end = panel * LANES, (panel + 1) * LANES
+            inverse = inverse_factor(gram_ref[start:end, start:end])
+            columns = thrice(rows_ref[:, start:end], inverse, 1, 1)
+            rows_ref[:, start:end] = columns
+            if end < rank:
+                scaled = exact(inverse, gram_ref[start:end, end:], 1, 0)
+                gram_ref[end:, end:] -= exact(scaled, scaled, 0, 0)
+                rows_ref[:, end:] -= thrice(columns, scaled, 1, 0)
         return carry
 
     lax.fori_loop(0, ITERS, step, 0)
@@ -232,7 +243,6 @@
         scratch_shapes=[
             pltpu.VMEM((tokens, tokens), jnp.bfloat16),
             pltpu.VMEM((tokens, tokens), jnp.bfloat16),
-            pltpu.VMEM((tokens, rank), jnp.float32),
             pltpu.VMEM((tokens, rank), jnp.float32),
             pltpu.VMEM((rank, rank), jnp.float32),
         ],

time: 140 us -> 124 us (0.89)
  Pallas kernels: 134 us -> 119 us
    pallas_call x1, Pallas kernels: 83.9 us -> 68.3 us  [iterate(): pl.pallas_call(iterate_kernel, out_shape=jax.ShapeDtypeStruct((joint // l...]
where the time goes in v5:
time: 124 us; the launch traced here: 122 us
  Pallas kernels  119 us (96%)
  local copies, waits for them, and re-layouts  1.95 us (2%)
    pallas_call x1, Pallas kernels, iterate(): pl.pallas_call(iterate_kernel, out_shape=jax.ShapeDtypeStruct((joint // l...  68.3 us
    pallas_call x1, Pallas kernels, gather(): pl.pallas_call(functools.partial(gather_kernel, heads), out_shape=(jax.Sh...  41.2 us
    pallas_call x1, Pallas kernels, project(): pl.pallas_call(project_kernel, grid=(depth // chunk,), out_shape=(jax.Sha...  9.08 us

profile of v5, /device:TPU:9, one launch (start us, length us, event | category | flops | bytes accessed | tf_op | source)
XLA Modules:
  0.0 121.7 jit_solution(12964481932208982230)
XLA Ops:
  0.0 0.7 convert_bitcast_fusion
  0.7 0.3 fusion
  1.0 0.1 pad_maximum_fusion
  1.1 0.0 copy-start
  1.1 9.1 %shard_map.64 = (f32[256,512]{1,0:T(8,128)}, f32[256,128]{1,0:T(8,128)}) custom-call(bf16[256,8192]{1,0:T(8,128)(2,1)} %bitcast.4, f32[1,8192]{1,0:T(1,128)} %bitcast.5, bf16[8192,256]{1,0:T(8,128)(2,1)} %key_ref.1, bf16[8192,256]{1,0:T(8,128)(2,1)} %value_ref.1), custom_call_target="tpu_custom_call" | custom-call | tf_op jit(solution)/shard_map/pallas_call | solution.py:276
  10.2 0.0 copy-done
  10.2 0.0 copy-start.1
  10.2 1.0 copy-done.1
  11.2 0.0 copy-start.2
  11.2 0.9 copy-done.2
  12.1 41.2 %shard_map.65 = (bf16[1024,2048]{1,0:T(8,128)(2,1)S(1)}, f32[2048,256]{1,0:T(8,128)S(1)}) custom-call(f32[256,512]{1,0:T(8,128)S(1)} %copy-done.1, f32[256,128]{1,0:T(8,128)S(1)} %copy-done.2, f32[128,128]{1,0:T(8,128)S(1)} %get-tuple-element.16.cosine_ref, f32[128,128]{1,0:T(8,128)S(1)} %get-tuple-element.17.sine_ref, f32[512,256]{1,0:T(8,128)S(1)} %copy-done), custom_call_target="tpu_custom_call" | custom-call | tf_op jit(solution)/shard_map/pallas_call | solution.py:452
  53.4 68.3 %shard_map.66 = f32[512,256]{1,0:T(8,128)} custom-call(bf16[1024,2048]{1,0:T(8,128)(2,1)S(1)} %get-tuple-element.11.joint_ref, f32[2048,256]{1,0:T(8,128)S(1)} %get-tuple-element.12.basis_ref), custom_call_target="tpu_custom_call" | custom-call | tf_op jit(solution)/shard_map/pallas_call | solution.py:238
  (1 shorter events, 0.0 us)
Async XLA Ops:
  1.1 9.1 %copy-start = (f32[512,256]{1,0:T(8,128)S(1)}, f32[512,256]{1,0:T(8,128)}, u32[]{:S(2)}) copy-start(f32[512,256]{1,0:T(8,128)} %basis_ref.1) | copy-start | bytes 1572868
  10.2 1.0 copy-start.1
  11.2 0.9 copy-start.2
